TPU v7x, 128 devices: a whole 4x4x4 slice. The times are simulated.
128 devices in a mesh: grp: 4 (over x), blk: 32 (over z, y, core).
Axes of the slice: x: 4, y: 4, z: 4, core: 2. Of those that a mesh axis runs over, the one named last changes fastest.
Arguments:
- inv_factor: bfloat16 [768, 384, 384], P(('grp', 'blk')), may hold values from -0.3125 to 0.3125
- coupling: bfloat16 [768, 384, 768], P(('grp', 'blk')), may hold values from -0.75 to 0.75
- boundary: bfloat16 [768, 768, 768], P(('grp', 'blk')), may hold values from -6 to 6
- load_int: bfloat16 [768, 384], P(('grp', 'blk')), may hold values from -6 to 6
- load_bnd: bfloat16 [768, 768], P(('grp', 'blk')), may hold values from -6 to 6
- counts: int32 [128], P(('grp', 'blk')), may hold values from 1 to 6, 512 in all
- tile_owner: int32 [768, 36, 1], P(('grp', 'blk')), may hold values from 0 to 127; in each aligned block of 216 rows (0 to 215, 216 to 431, ..., all dimensions but the last counted through in order) at most 2 rows name the same one
- tile_slot: int32 [768, 36], P(('grp', 'blk')), may hold values from 0 to 63
- vec_owner: int32 [768, 6, 1], P(('grp', 'blk')), may hold values from 0 to 127; in each aligned block of 36 rows (0 to 35, 36 to 71, ..., all dimensions but the last counted through in order) at most 2 rows name the same one
- vec_slot: int32 [768, 6], P(('grp', 'blk')), may hold values from 0 to 15
Outputs:
- assembled: float32 [8192, 128, 128], P(('grp', 'blk'))
- loads: float32 [2048, 128], P(('grp', 'blk'))
Inputs may be any that keep to these rules, and one draw needn't show every extreme that they name: `tile_owner`: among the 216 rows of one device, no owner is named by more than 2 tiles. `vec_owner`: among the 36 rows of one device, no owner is named by more than 2 load blocks.
All inputs are finite; a program needn't handle non-finite values. No bound on the sum of `counts` on one device may be relied on, other than what follows from the above.
Results may differ from a plain program's by a relative error of at most 0.004.
Values may be sent and summed in bfloat16 or wider, within the bound.
No kernel may reach another device: no remote copies, remote signals or barrier semaphores. Data moves between devices by JAX's collectives and lax.ppermute only.
A program may use at most 128 MiB of HBM per device.

v0:
```python
import jax
import jax.numpy as jnp
from jax import lax
from jax.sharding import PartitionSpec as P

BLOCK_UNKNOWNS = 128
SLOT_DEV = 64
VSLOT_DEV = 16


def placement(owner, peers, room):
    count = owner.shape[0]
    hits = (owner[:, None] == jnp.arange(peers, dtype=jnp.int32)[None, :]).astype(jnp.int32)
    rank = jnp.sum(jnp.cumsum(hits, axis=0) * hits, axis=1) - 1
    target = owner * room + rank
    return (
        jnp.full((peers * room,), count, jnp.int32)
        .at[target]
        .set(jnp.arange(count, dtype=jnp.int32))
    )


def packed(rows, slots, source):
    padded_rows = jnp.concatenate([rows, jnp.zeros((1, rows.shape[1]), rows.dtype)], axis=0)
    padded_ids = jnp.concatenate([slots, jnp.full((1,), -1, jnp.int32)])
    return (padded_rows[source], padded_ids[source])


def summed(rows, ids, count):
    select = (ids[None, :] == jnp.arange(count, dtype=jnp.int32)[:, None]).astype(rows.dtype)
    return jnp.dot(select, rows, preferred_element_type=jnp.float32)


def shards(
    inv_factor,
    coupling,
    boundary,
    load_int,
    load_bnd,
    counts,
    tile_owner,
    tile_slot,
    vec_owner,
    vec_slot,
):
    emax = inv_factor.shape[0]
    nb = boundary.shape[1]
    tile = BLOCK_UNKNOWNS
    tiles = nb // tile
    element_groups = lax.axis_size("grp")
    columns = lax.axis_size("blk")
    peers = element_groups * columns
    ntiles = emax * tiles * tiles
    room = max(2, 3 * ntiles // (2 * peers))
    vroom = max(2, 3 * emax * tiles // (2 * peers))

    def condense(slot_index, carry):
        stiffness_matrices, load_vectors = carry
        factor = lax.dynamic_index_in_dim(inv_factor, slot_index, 0, keepdims=False)
        couple = lax.dynamic_index_in_dim(coupling, slot_index, 0, keepdims=False)
        bound = lax.dynamic_index_in_dim(boundary, slot_index, 0, keepdims=False)
        inner = lax.dynamic_index_in_dim(load_int, slot_index, 0, keepdims=False)
        outer = lax.dynamic_index_in_dim(load_bnd, slot_index, 0, keepdims=False)
        coupled = jnp.dot(factor, couple, preferred_element_type=jnp.float32).astype(jnp.bfloat16)
        product = lax.dot_general(
            coupled, coupled, (((0,), (0,)), ((), ())), preferred_element_type=jnp.float32
        )
        schur = (bound.astype(jnp.float32) - product).astype(jnp.bfloat16)
        pulled = jnp.dot(factor, inner, preferred_element_type=jnp.float32).astype(jnp.bfloat16)
        condensed = (
            outer.astype(jnp.float32) - jnp.dot(pulled, coupled, preferred_element_type=jnp.float32)
        ).astype(jnp.bfloat16)
        stiffness_matrices = lax.dynamic_update_index_in_dim(
            stiffness_matrices, schur, slot_index, 0
        )
        load_vectors = lax.dynamic_update_index_in_dim(load_vectors, condensed, slot_index, 0)
        return (stiffness_matrices, load_vectors)

    start_offset = (jnp.zeros((emax, nb, nb), jnp.bfloat16), jnp.zeros((emax, nb), jnp.bfloat16))
    stiffness_matrices, load_vectors = lax.fori_loop(0, counts[0], condense, start_offset)
    pieces = (
        stiffness_matrices.reshape(emax, tiles, tile, tiles, tile)
        .transpose(0, 1, 3, 2, 4)
        .reshape(ntiles, tile * tile)
    )
    blocks = load_vectors.reshape(emax * tiles, tile)
    source = placement(tile_owner.reshape(-1), peers, room)
    vsource = placement(vec_owner.reshape(-1), peers, vroom)
    send_tiles, send_ids = packed(pieces, tile_slot.reshape(-1), source)
    send_blocks, send_vids = packed(blocks, vec_slot.reshape(-1), vsource)
    first = (
        lax.all_to_all(
            send_tiles.reshape(element_groups, columns * room, tile * tile),
            "grp",
            split_axis=0,
            concat_axis=0,
            tiled=True,
        ),
        lax.all_to_all(
            send_ids.reshape(element_groups, columns * room),
            "grp",
            split_axis=0,
            concat_axis=0,
            tiled=True,
        ),
        lax.all_to_all(
            send_blocks.reshape(element_groups, columns * vroom, tile),
            "grp",
            split_axis=0,
            concat_axis=0,
            tiled=True,
        ),
        lax.all_to_all(
            send_vids.reshape(element_groups, columns * vroom),
            "grp",
            split_axis=0,
            concat_axis=0,
            tiled=True,
        ),
    )
    second = (
        lax.all_to_all(
            first[0].reshape(element_groups, columns, room, tile * tile),
            "blk",
            split_axis=1,
            concat_axis=1,
            tiled=True,
        ),
        lax.all_to_all(
            first[1].reshape(element_groups, columns, room),
            "blk",
            split_axis=1,
            concat_axis=1,
            tiled=True,
        ),
        lax.all_to_all(
            first[2].reshape(element_groups, columns, vroom, tile),
            "blk",
            split_axis=1,
            concat_axis=1,
            tiled=True,
        ),
        lax.all_to_all(
            first[3].reshape(element_groups, columns, vroom),
            "blk",
            split_axis=1,
            concat_axis=1,
            tiled=True,
        ),
    )
    received_tiles, got_ids, got_blocks, got_vids = second
    received_tiles = received_tiles.reshape(peers * room, tile * tile)
    got_ids = got_ids.reshape(peers * room)
    got_blocks = got_blocks.reshape(peers * vroom, tile)
    got_vids = got_vids.reshape(peers * vroom)
    assembled = summed(received_tiles, got_ids, SLOT_DEV).reshape(SLOT_DEV, tile, tile)
    loads = summed(got_blocks, got_vids, VSLOT_DEV)
    return (assembled, loads)


def solution(mesh):
    in_specs = (
        P(("grp", "blk"), None, None),
        P(("grp", "blk"), None, None),
        P(("grp", "blk"), None, None),
        P(("grp", "blk"), None),
        P(("grp", "blk"), None),
        P(("grp", "blk")),
        P(("grp", "blk"), None, None),
        P(("grp", "blk"), None),
        P(("grp", "blk"), None, None),
        P(("grp", "blk"), None),
    )
    out_specs = (P(("grp", "blk"), None, None), P(("grp", "blk"), None))
    return jax.shard_map(shards, mesh=mesh, in_specs=in_specs, out_specs=out_specs, check_vma=False)
```

profile of v0, /device:TPU:0, one launch (start us, length us, event | category | flops | bytes accessed | tf_op | source)
XLA Modules:
  0.0 462.7 jit_solution(5549566680859100574)
XLA Ops:
  4.7 22.6 %compare_select_fusion.4 = s32[256]{0:T(256)S(1)} fusion(s32[]{:T(128)} %bitcast.21, s32[]{:T(128)} %bitcast.22, s32[]{:T(128)} %bitcast.23, s32[]{:T(128)} %bitcast.24, s32[]{:T(128)} %bitcast.25, s32[]{:T(128)} %bitcast.26, s32[]{:T(128)} %bitcast.27, s32[]{:T(128)} %bitcast.28, s32[]{:T(128)} %bitcast.29, s32[]{:T(128)} %bitcast.30, s32[]{:T(128)} %bitcast.31, ...), kind=kLoop, calls=%fused_computation.51 | loop fusion | flops 19200 | bytes 2192 | tf_op jit(solution)/shard_map/gather | solution.py:26
  28.0 4.4 all-to-all-start.4
  38.6 4.8 %all-to-all-start = ((s32[4,1,64]{2,1,0:T(1,128)}), s32[4,1,64]{2,1,0:T(1,128)S(1)}, u32[]{:S(2)}, u32[]{:S(2)}) async-start(s32[4,1,64]{2,1,0:T(1,128)} %bitcast.10), calls=%async_computation | async-start | bytes 4096 | tf_op jit(solution)/shard_map/all_to_all | solution.py:99
  43.4 3.3 broadcast_in_dim.38
  46.7 46.6 %while.12 = (s32[]{:T(128)}, bf16[6,768,768]{2,1,0:T(8,128)(2,1)}, bf16[6,768]{1,0:T(8,128)(2,1)S(1)}, s32[]{:T(128)}, bf16[6,768,768]{2,1,0:T(8,128)(2,1)}, /*i...) while((s32[]{:T(128)}, bf16[6,768,768]{2,1,0:T(8,128)(2,1)}, ...), condition=%wide.region_5.6_spmd, body=%wide.region_4.5_spmd.sunk | while | flops 682428672 | bytes 5926571 | solution.py:80
  58.8 3.1 fusion.55
  66.5 3.1 fusion.55
  74.2 3.1 fusion.55
  81.9 3.1 fusion.55
  89.5 3.1 fusion.55
  94.0 6.9 %all-to-all-start.5 = ((s32[4,32,2]{0,2,1:T(2,128)}), s32[4,32,2]{0,2,1:T(2,128)S(1)}, u32[]{:S(2)}, u32[]{:S(2)}) async-start(s32[4,32,2]{0,2,1:T(2,128)} %bitcast.58), calls=%async_computation.5 | async-start | bytes 65536 | tf_op jit(solution)/shard_map/all_to_all | solution.py:143
  101.7 6.7 %all-to-all-done.5 = s32[4,32,2]{0,2,1:T(2,128)S(1)} async-done(((s32[4,32,2]{0,2,1:T(2,128)}), s32[4,32,2]{0,2,1:T(2,128)S(1)}, u32[]{:S(2)}, u32[]{:S(2)}) %all-to-all-start.5) | async-done | bytes 1056 | tf_op jit(solution)/shard_map/all_to_all | solution.py:143
  108.4 3.9 all-to-all-start.1
  113.8 5.9 %all-to-all-done.1 = s32[4,32,2]{0,2,1:T(2,128)S(1)} async-done(((s32[4,32,2]{0,2,1:T(2,128)}), s32[4,32,2]{0,2,1:T(2,128)S(1)}, u32[]{:S(2)}, u32[]{:S(2)}) %all-to-all-start.1) | async-done | bytes 1056 | tf_op jit(solution)/shard_map/all_to_all | solution.py:129
  119.6 5.9 %all-to-all-start.6 = ((bf16[4,64,128]{2,1,0:T(8,128)(2,1)}), bf16[4,64,128]{2,1,0:T(8,128)(2,1)S(1)}, u32[]{:S(2)}, u32[]{:S(2)}) async-start(bf16[4,64,128]{2,1,0:T(8,128)(2,1)} %bitcast.59), calls=%async_computation.6 | async-start | bytes 131072 | tf_op jit(solution)/shard_map/all_to_all | solution.py:106
  125.5 15.4 %reshape.146 = bf16[6,6,128,6,128]{4,3,2,1,0:T(8,128)(2,1)} reshape(bf16[6,768,768]{2,1,0:T(8,128)(2,1)} %get-tuple-element.51) | data formatting | bytes 14155776 | tf_op jit(solution)/shard_map/reshape | solution.py:82
  141.0 8.7 %copy.64 = bf16[6,6,6,128,128]{4,3,2,1,0:T(8,128)(2,1)} copy(bf16[6,6,6,128,128]{4,2,3,1,0:T(8,128)(2,1)} %bitcast.120) | data formatting | bytes 14155776 | tf_op jit(solution)/shard_map/transpose | solution.py:83
  149.7 9.6 %copy.79 = bf16[27,8,128,128]{3,1,2,0:T(8,128)(2,1)S(1)} copy(bf16[27,8,128,128]{3,2,1,0:T(8,128)(2,1)} %bitcast.126) | data formatting | bytes 14155776
  159.2 3.8 concatenate.13
  163.0 20.6 %gather_fusion.1 = bf16[256,16384]{1,0:T(8,128)(2,1)} fusion(bf16[217,16384]{1,0:T(8,128)(2,1)} %concatenate.13, s32[1024]{0:T(1024)S(1)} %pad_clamp_fusion.1), kind=kCustom, calls=%fused_computation.1 | custom fusion | bytes 16778240 | tf_op jit(solution)/shard_map/gather | solution.py:26
  183.6 5.7 %all-to-all-start.2 = ((bf16[4,64,16384]{2,1,0:T(8,128)(2,1)}), bf16[4,64,16384]{2,1,0:T(8,128)(2,1)}, u32[]{:S(2)}, u32[]{:S(2)}) async-start(bf16[4,64,16384]{2,1,0:T(8,128)(2,1)} %bitcast.121), calls=%async_computation.2 | async-start | bytes 16777216 | tf_op jit(solution)/shard_map/all_to_all | solution.py:92
  190.0 93.4 %all-to-all-done.2 = bf16[4,64,16384]{2,1,0:T(8,128)(2,1)} async-done(((bf16[4,64,16384]{2,1,0:T(8,128)(2,1)}), bf16[4,64,16384]{2,1,0:T(8,128)(2,1)}, u32[]{:S(2)}, u32[]{:S(2)}) %all-to-all-start.2) | async-done | bytes 8388640 | tf_op jit(solution)/shard_map/all_to_all | solution.py:92
  283.4 4.1 all-to-all-start.7
  287.5 10.1 %copy.65 = bf16[4,64,16384]{2,0,1:T(4,128)(2,1)S(1)} copy(bf16[4,64,16384]{2,1,0:T(8,128)(2,1)} %all-to-all-done.2) | data formatting | bytes 16777216 | tf_op jit(solution)/shard_map/all_to_all | solution.py:92
  297.6 7.7 %copy.66 = bf16[4,32,2,16384]{3,2,0,1:T(2,128)(2,1)} copy(bf16[4,32,2,16384]{3,0,2,1:T(4,128)(2,1)S(1)} %bitcast.123) | data formatting | bytes 16777216 | tf_op jit(solution)/shard_map/reshape | solution.py:123
  305.3 7.6 %all-to-all-start.3 = ((bf16[4,32,2,16384]{3,2,0,1:T(2,128)(2,1)}), bf16[4,32,2,16384]{3,2,0,1:T(2,128)(2,1)}, u32[]{:S(2)}, u32[]{:S(2)}) async-start(bf16[4,32,2,16384]{3,2,0,1:T(2,128)(2,1)} %copy.66), calls=%async_computation.3 | async-start | bytes 16777216 | tf_op jit(solution)/shard_map/all_to_all | solution.py:122
  314.7 104.1 %all-to-all-done.3 = bf16[4,32,2,16384]{3,2,0,1:T(2,128)(2,1)} async-done(((bf16[4,32,2,16384]{3,2,0,1:T(2,128)(2,1)}), bf16[4,32,2,16384]{3,2,0,1:T(2,128)(2,1)}, u32[]{:S(2)}, u32[]{:S(2)}) %all-to-all-start.3) | async-done | bytes 8388640 | tf_op jit(solution)/shard_map/all_to_all | solution.py:122
  418.8 8.0 %copy.67 = bf16[4,32,2,16384]{3,2,1,0:T(2,128)(2,1)} copy(bf16[4,32,2,16384]{3,2,0,1:T(2,128)(2,1)} %all-to-all-done.3) | data formatting | bytes 16777216 | tf_op jit(solution)/shard_map/all_to_all | solution.py:122
  426.9 13.1 %reshape.150 = bf16[256,16384]{1,0:T(8,128)(2,1)} reshape(bf16[4,32,2,16384]{3,2,1,0:T(2,128)(2,1)} %copy.67) | data formatting | bytes 16777216 | tf_op jit(solution)/shard_map/reshape | solution.py:152
  440.0 11.9 %copy.68 = bf16[16384,256]{1,0:T(8,128)(2,1)} copy(bf16[16384,256]{0,1:T(8,128)(2,1)} %bitcast.124) | data formatting | bytes 16777216 | tf_op jit(solution)/shard_map/dot_general | solution.py:31
  451.8 6.0 %fusion.17 = f32[64,128,128]{2,0,1:T(8,128)S(1)} fusion(bf16[128,128,256]{2,1,0:T(8,128)(2,1)} %bitcast.122, s32[256]{0:T(256)S(1)} %eq.74), kind=kOutput, calls=%fused_computation.35 | convolution fusion | flops 536887296 | bytes 12583936 | tf_op jit(solution)/shard_map/dot_general | solution.py:31
  457.8 4.4 copy.74
  (104 shorter events, 42.2 us)
Async XLA Ops:
  28.0 10.6 %all-to-all-start.4 = ((s32[4,1,64]{2,1,0:T(1,128)}), s32[4,1,64]{2,1,0:T(1,128)S(1)}, u32[]{:S(2)}, u32[]{:S(2)}) async-start(s32[4,1,64]{2,1,0:T(1,128)} %bitcast.57), calls=%async_computation.4 | async-start | bytes 4096 | tf_op jit(solution)/shard_map/all_to_all | solution.py:113
  38.6 55.4 %all-to-all-start = ((s32[4,1,64]{2,1,0:T(1,128)}), s32[4,1,64]{2,1,0:T(1,128)S(1)}, u32[]{:S(2)}, u32[]{:S(2)}) async-start(s32[4,1,64]{2,1,0:T(1,128)} %bitcast.10), calls=%async_computation | async-start | bytes 4096 | tf_op jit(solution)/shard_map/all_to_all | solution.py:99
  94.0 14.4 %all-to-all-start.5 = ((s32[4,32,2]{0,2,1:T(2,128)}), s32[4,32,2]{0,2,1:T(2,128)S(1)}, u32[]{:S(2)}, u32[]{:S(2)}) async-start(s32[4,32,2]{0,2,1:T(2,128)} %bitcast.58), calls=%async_computation.5 | async-start | bytes 65536 | tf_op jit(solution)/shard_map/all_to_all | solution.py:143
  108.4 11.3 %all-to-all-start.1 = ((s32[4,32,2]{0,2,1:T(2,128)}), s32[4,32,2]{0,2,1:T(2,128)S(1)}, u32[]{:S(2)}, u32[]{:S(2)}) async-start(s32[4,32,2]{0,2,1:T(2,128)} %bitcast.11), calls=%async_computation.1 | async-start | bytes 65536 | tf_op jit(solution)/shard_map/all_to_all | solution.py:129
  119.6 64.0 %all-to-all-start.6 = ((bf16[4,64,128]{2,1,0:T(8,128)(2,1)}), bf16[4,64,128]{2,1,0:T(8,128)(2,1)S(1)}, u32[]{:S(2)}, u32[]{:S(2)}) async-start(bf16[4,64,128]{2,1,0:T(8,128)(2,1)} %bitcast.59), calls=%async_computation.6 | async-start | bytes 131072 | tf_op jit(solution)/shard_map/all_to_all | solution.py:106
  183.6 99.8 %all-to-all-start.2 = ((bf16[4,64,16384]{2,1,0:T(8,128)(2,1)}), bf16[4,64,16384]{2,1,0:T(8,128)(2,1)}, u32[]{:S(2)}, u32[]{:S(2)}) async-start(bf16[4,64,16384]{2,1,0:T(8,128)(2,1)} %bitcast.121), calls=%async_computation.2 | async-start | bytes 16777216 | tf_op jit(solution)/shard_map/all_to_all | solution.py:92
  283.4 21.9 %all-to-all-start.7 = ((bf16[4,32,2,128]{3,2,0,1:T(2,128)(2,1)}), bf16[4,32,2,128]{3,2,0,1:T(2,128)(2,1)S(1)}, u32[]{:S(2)}, u32[]{:S(2)}) async-start(bf16[4,32,2,128]{3,2,0,1:T(2,128)(2,1)} %copy.72), calls=%async_computation.7 | async-start | bytes 131072 | tf_op jit(solution)/shard_map/all_to_all | solution.py:136
  305.3 113.5 %all-to-all-start.3 = ((bf16[4,32,2,16384]{3,2,0,1:T(2,128)(2,1)}), bf16[4,32,2,16384]{3,2,0,1:T(2,128)(2,1)}, u32[]{:S(2)}, u32[]{:S(2)}) async-start(bf16[4,32,2,16384]{3,2,0,1:T(2,128)(2,1)} %copy.66), calls=%async_computation.3 | async-start | bytes 16777216 | tf_op jit(solution)/shard_map/all_to_all | solution.py:122
where the time goes:
time: 471 us; the launch traced here: 463 us
  waiting for transfers between devices  210 us (45%)
  local copies, waits for them, and re-layouts  130 us (28%)
  matrix products  43.6 us (9%)
  starting transfers between devices  43.3 us (9%)
  other arithmetic  29.3 us (6%)
  loops' own time  4.92 us (1%)
    all_to_all x1, waiting for transfers between devices, shards(): lax.all_to_all(first[0].reshape(element_groups, columns, room, tile * til...  104 us
    all_to_all x1, waiting for transfers between devices, shards(): lax.all_to_all(send_tiles.reshape(element_groups, columns * room, tile *...  93.4 us
    gather x5, local copies, waits for them, and re-layouts, packed(): return (padded_rows[source], padded_ids[source])  25.4 us
    gather x3, other arithmetic, packed(): return (padded_rows[source], padded_ids[source])  22.6 us
    dot_general x6, matrix products, condense(): lax.dot_general(coupled, coupled, (((0,), (0,)), ((), ())), preferred_ele...  18.7 us
    reshape x1, local copies, waits for them, and re-layouts, shards(): stiffness_matrices.reshape(emax, tiles, tile, tiles, tile)  15.4 us
    unnamed x3, local copies, waits for them, and re-layouts  14 us
    reshape x1, local copies, waits for them, and re-layouts, shards(): received_tiles = received_tiles.reshape(peers * room, tile * tile)  13.1 us
  transfers between devices with their start and end apart: 8, of which 4 were waited for; matrix products, arithmetic and copies ran while one was open for 28% of the time, Pallas kernels for 0%

commit v1 on v0

v1 whole, which is shorter than its diff:
```python
import jax
import jax.numpy as jnp
from jax import lax
from jax.experimental import pallas as pl
from jax.experimental.pallas import tpu as pltpu
from jax.sharding import PartitionSpec as P

TILE = 128
SLOT_DEV = 64
VSLOT_DEV = 16
CAP = 2
HEAD = 8
AXES = ("grp", "blk")
MIB = 1 << 20


def spread(value):
    return jnp.full((1, TILE), value, jnp.int32).astype(jnp.float32)


def row_of(ref, k):
    rows = ref[...].astype(jnp.float32)
    at = lax.broadcasted_iota(jnp.int32, rows.shape, 0) == k
    return jnp.sum(jnp.where(at, rows, 0.0), axis=0, keepdims=True)


def pack_kernel(
    counts,
    owner,
    slot,
    vowner,
    vslot,
    factor_hbm,
    couple_hbm,
    bound_hbm,
    inner,
    outer,
    send,
    factor,
    couple,
    bound,
    pieces,
    left,
    head,
    head16,
    used,
    vused,
    target,
    vtarget,
    in_sem,
    out_sem,
    head_sem,
):
    emax, ni, nb = couple.shape
    tiles = nb // TILE
    per = tiles * tiles
    peers = used.shape[0]
    live = counts[0]

    def loads(k):
        return (
            pltpu.make_async_copy(factor_hbm.at[k], factor.at[k], in_sem.at[0, k]),
            pltpu.make_async_copy(couple_hbm.at[k], couple.at[k], in_sem.at[1, k]),
            pltpu.make_async_copy(bound_hbm.at[k], bound.at[k], in_sem.at[2, k]),
        )

    @pl.loop(0, live)
    def _(k):
        for copy in loads(k):
            copy.start()

    row = lax.broadcasted_iota(jnp.int32, (HEAD, TILE), 0)
    blank = jnp.where((row >= CAP) & (row < 3 * CAP), -1.0, 0.0).astype(jnp.float32)

    @pl.loop(0, peers)
    def _(p):
        used[p] = 0
        vused[p] = 0
        head[pl.ds(pl.multiple_of(p * HEAD, HEAD), HEAD), :] = blank

    @pl.loop(0, live)
    def _(k):
        @pl.loop(0, per)
        def _(t):
            p = owner[k, 0, t]
            r = used[p]
            used[p] = r + 1
            target[k * per + t] = p * CAP + r
            head[pl.ds(p * HEAD + CAP + r, 1), :] = spread(slot[k, t])

        @pl.loop(0, tiles)
        def _(t):
            p = vowner[k, 0, t]
            r = vused[p]
            vused[p] = r + 1
            vtarget[k * tiles + t] = p * HEAD + r
            head[pl.ds(p * HEAD + 2 * CAP + r, 1), :] = spread(vslot[k, t])

    @pl.loop(0, live)
    def _(k):
        for copy in loads(k):
            copy.wait()
        coupled = lax.dot_general(
            couple[k], factor[k], (((0,), (1,)), ((), ())), preferred_element_type=jnp.float32
        ).astype(jnp.bfloat16)
        inner_rows = jnp.broadcast_to(row_of(inner, k), (16, ni)).astype(jnp.bfloat16)
        pulled = lax.dot_general(
            inner_rows, factor[k], (((1,), (1,)), ((), ())), preferred_element_type=jnp.float32
        ).astype(jnp.bfloat16)
        left[pl.ds(0, nb), :] = coupled
        left[pl.ds(nb, 16), :] = pulled
        for a in range(tiles):
            last = a == tiles - 1
            lhs = left[pl.ds(a * TILE, TILE + (16 if last else 0)), :]
            product = lax.dot_general(
                lhs, left[pl.ds(0, nb), :], (((1,), (1,)), ((), ())), preferred_element_type=jnp.float32
            )
            schur = bound[k, pl.ds(a * TILE, TILE), :].astype(jnp.float32) - product[:TILE]
            for b in range(tiles):
                pieces[k, a * tiles + b] = schur[:, b * TILE : (b + 1) * TILE].astype(jnp.bfloat16)
                t = k * per + a * tiles + b
                to = target[t]
                peer = lax.shift_right_logical(to, 1)
                start = pl.multiple_of(HEAD + (to & 1) * TILE, HEAD)
                pltpu.make_async_copy(
                    pieces.at[k, a * tiles + b], send.at[peer, pl.ds(start, TILE), :], out_sem.at[k]
                ).start()
            if last:
                condensed = row_of(outer, k) - product[TILE : TILE + 1]
                for b in range(tiles):
                    head[pl.ds(vtarget[k * tiles + b], 1), :] = condensed[:, b * TILE : (b + 1) * TILE]

    head16[...] = head[...].reshape(peers, HEAD, TILE).astype(jnp.bfloat16)
    head_copy = pltpu.make_async_copy(head16, send.at[:, pl.ds(0, HEAD), :], head_sem)
    head_copy.start()

    @pl.loop(0, live)
    def _(k):
        pltpu.make_async_copy(pieces.at[k], pieces.at[k], out_sem.at[k]).wait()

    head_copy.wait()


def packed(peers, inv_factor, coupling, boundary, load_int, load_bnd, counts, owner, slot, vowner, vslot):
    emax, ni, nb = coupling.shape
    tiles = nb // TILE
    per = tiles * tiles
    smem = pl.BlockSpec(memory_space=pltpu.SMEM)
    hbm = pl.BlockSpec(memory_space=pltpu.HBM)
    vmem = pl.BlockSpec(memory_space=pltpu.VMEM)
    return pl.pallas_call(
        pack_kernel,
        out_shape=jax.ShapeDtypeStruct((peers, HEAD + CAP * TILE, TILE), jnp.bfloat16),
        in_specs=[smem] * 5 + [hbm] * 3 + [vmem] * 2,
        out_specs=hbm,
        scratch_shapes=[
            pltpu.VMEM((emax, ni, ni), jnp.bfloat16),
            pltpu.VMEM((emax, ni, nb), jnp.bfloat16),
            pltpu.VMEM((emax, nb, nb), jnp.bfloat16),
            pltpu.VMEM((emax, per, TILE, TILE), jnp.bfloat16),
            pltpu.VMEM((nb + 16, ni), jnp.bfloat16),
            pltpu.VMEM((peers * HEAD, TILE), jnp.float32),
            pltpu.VMEM((peers, HEAD, TILE), jnp.bfloat16),
            pltpu.SMEM((peers,), jnp.int32),
            pltpu.SMEM((peers,), jnp.int32),
            pltpu.SMEM((emax * per,), jnp.int32),
            pltpu.SMEM((emax * tiles,), jnp.int32),
            pltpu.SemaphoreType.DMA((3, emax)),
            pltpu.SemaphoreType.DMA((emax,)),
            pltpu.SemaphoreType.DMA,
        ],
        compiler_params=pltpu.CompilerParams(vmem_limit_bytes=48 * MIB),
        name="condense_pack",
    )(
        counts,
        owner,
        slot,
        vowner,
        vslot,
        inv_factor,
        coupling,
        boundary,
        load_int,
        load_bnd,
    )


def sum_kernel(got, assembled, loads, head, parts, ids_vec, ids, head_sem, part_sem, ids_sem):
    peers = head.shape[0]
    chunks, width = parts.shape[:2]
    head_copy = pltpu.make_async_copy(got.at[:, pl.ds(0, HEAD), :], head, head_sem)
    head_copy.start()
    for c in range(chunks):
        pltpu.make_async_copy(
            got.at[pl.ds(c * width, width), pl.ds(HEAD, CAP * TILE), :], parts.at[c], part_sem.at[c]
        ).start()

    zero = jnp.zeros((TILE, TILE), jnp.float32)

    @pl.loop(0, SLOT_DEV)
    def _(s):
        assembled[s] = zero

    head_copy.wait()
    rows = head[...].astype(jnp.float32)
    diagonal = lax.broadcasted_iota(jnp.int32, (peers, TILE), 0) == lax.broadcasted_iota(
        jnp.int32, (peers, TILE), 1
    )
    lane = lax.broadcasted_iota(jnp.int32, (peers, TILE), 1).astype(jnp.float32)
    total = jnp.zeros((TILE, TILE), jnp.float32)
    for r in range(CAP):
        named = jnp.where(diagonal, rows[:, CAP + r, :], 0.0)
        ids_vec[pl.ds(r, 1), :] = jnp.sum(named, axis=0, keepdims=True).astype(jnp.int32)
        select = (rows[:, 2 * CAP + r, :] == lane).astype(jnp.bfloat16)
        total += lax.dot_general(
            select,
            rows[:, r, :].astype(jnp.bfloat16),
            (((0,), (0,)), ((), ())),
            preferred_element_type=jnp.float32,
        )
    ids_copy = pltpu.make_async_copy(ids_vec, ids, ids_sem)
    ids_copy.start()
    loads[...] = total[:VSLOT_DEV]
    ids_copy.wait()

    for c in range(chunks):
        pltpu.make_async_copy(
            got.at[pl.ds(c * width, width), pl.ds(HEAD, CAP * TILE), :], parts.at[c], part_sem.at[c]
        ).wait()

        @pl.loop(0, width)
        def _(w):
            for r in range(CAP):
                s = ids[r, c * width + w]

                @pl.when(s >= 0)
                def _():
                    assembled[s] += parts[c, w, pl.ds(r * TILE, TILE), :].astype(jnp.float32)


def summed(got):
    peers = got.shape[0]
    chunks = 8
    hbm = pl.BlockSpec(memory_space=pltpu.HBM)
    vmem = pl.BlockSpec(memory_space=pltpu.VMEM)
    return pl.pallas_call(
        sum_kernel,
        out_shape=(
            jax.ShapeDtypeStruct((SLOT_DEV, TILE, TILE), jnp.float32),
            jax.ShapeDtypeStruct((VSLOT_DEV, TILE), jnp.float32),
        ),
        in_specs=[hbm],
        out_specs=(vmem, vmem),
        scratch_shapes=[
            pltpu.VMEM((peers, HEAD, TILE), jnp.bfloat16),
            pltpu.VMEM((chunks, peers // chunks, CAP * TILE, TILE), jnp.bfloat16),
            pltpu.VMEM((8, TILE), jnp.int32),
            pltpu.SMEM((8, TILE), jnp.int32),
            pltpu.SemaphoreType.DMA,
            pltpu.SemaphoreType.DMA((chunks,)),
            pltpu.SemaphoreType.DMA,
        ],
        compiler_params=pltpu.CompilerParams(vmem_limit_bytes=48 * MIB),
        name="sum_tiles",
    )(got)


def shards(
    inv_factor, coupling, boundary, load_int, load_bnd, counts, tile_owner, tile_slot, vec_owner, vec_slot
):
    peers = lax.axis_size("grp") * lax.axis_size("blk")
    send = packed(
        peers,
        inv_factor,
        coupling,
        boundary,
        load_int,
        load_bnd,
        counts,
        jnp.swapaxes(tile_owner, 1, 2),
        tile_slot,
        jnp.swapaxes(vec_owner, 1, 2),
        vec_slot,
    )
    got = lax.all_to_all(send, AXES, split_axis=0, concat_axis=0, tiled=True)
    return summed(got)


def solution(mesh):
    in_specs = (
        P(AXES, None, None),
        P(AXES, None, None),
        P(AXES, None, None),
        P(AXES, None),
        P(AXES, None),
        P(AXES),
        P(AXES, None, None),
        P(AXES, None),
        P(AXES, None, None),
        P(AXES, None),
    )
    out_specs = (P(AXES, None, None), P(AXES, None))
    return jax.shard_map(shards, mesh=mesh, in_specs=in_specs, out_specs=out_specs, check_vma=False)
```

time: 471 us -> 149 us (0.32); the launches traced: 463 us -> 147 us
  waiting for transfers between devices: 210 us -> 0 us
  local copies, waits for them, and re-layouts: 130 us -> 7.61 us
  blocking collectives: 0 us -> 119 us
  matrix products: 43.6 us -> 0 us
  starting transfers between devices: 43.3 us -> 0 us
  other arithmetic: 29.3 us -> 0 us
  Pallas kernels: 0 us -> 19.2 us
  loops' own time: 4.92 us -> 0 us
    all_to_all x8 -> x0, waiting for transfers between devices: 210 us -> none  [the longest x1 104 us: shards(): lax.all_to_all(first[0].reshape(element_groups, columns, room, tile * til...]
    all_to_all x0 -> x1, blocking collectives: none -> 119 us  [shards(): got = lax.all_to_all(send, AXES, split_axis=0, concat_axis=0, tiled=True)]
    dot_general x26 -> x0, matrix products: 43.6 us -> none  [the longest x6 18.7 us: condense(): lax.dot_general(coupled, coupled, (((0,), (0,)), ((), ())), preferred_ele...]
    all_to_all x8 -> x0, starting transfers between devices: 43.3 us -> none  [the longest x1 7.62 us: shards(): lax.all_to_all(first[0].reshape(element_groups, columns, room, tile * til...]
    reshape x7 -> x0, local copies, waits for them, and re-layouts: 38.5 us -> none  [the longest x1 15.4 us: shards(): stiffness_matrices.reshape(emax, tiles, tile, tiles, tile)]
    gather x5 -> x0, local copies, waits for them, and re-layouts: 25.4 us -> none  [packed(): return (padded_rows[source], padded_ids[source])]
    gather x3 -> x0, other arithmetic: 22.6 us -> none  [packed(): return (padded_rows[source], padded_ids[source])]
    all_to_all x9 -> x0, local copies, waits for them, and re-layouts: 21.5 us -> none  [the longest x1 10.1 us: shards(): lax.all_to_all(send_tiles.reshape(element_groups, columns * room, tile *...]
  transfers between devices with their start and end apart: 8 -> 0, of which waited for: 4 -> 0; matrix products, arithmetic and copies ran while one was open for 28% -> 0% of each run, Pallas kernels for 0% -> 0%
where the time goes in v1:
time: 149 us; the launch traced here: 147 us
  blocking collectives  119 us (80%)
  Pallas kernels  19.2 us (13%)
  local copies, waits for them, and re-layouts  7.61 us (5%)
    all_to_all x1, blocking collectives, shards(): got = lax.all_to_all(send, AXES, split_axis=0, concat_axis=0, tiled=True)  119 us
    pallas_call x1, Pallas kernels, summed(): pl.pallas_call(sum_kernel, out_shape=(jax.ShapeDtypeStruct((SLOT_DEV, TIL...  9.99 us
    pallas_call x1, Pallas kernels, packed(): pl.pallas_call(pack_kernel, out_shape=jax.ShapeDtypeStruct((peers, HEAD +...  9.25 us
    unnamed x16, local copies, waits for them, and re-layouts  7.61 us

profile of v1, /device:TPU:0, one launch (start us, length us, event | category | flops | bytes accessed | tf_op | source)
XLA Modules:
  0.0 147.4 jit_solution(1685852844475726431)
XLA Ops:
  1.3 0.0 copy-start
  1.3 2.0 %copy-done = bf16[6,384,768]{2,1,0:T(8,128)(2,1)S(1)} copy-done((bf16[6,384,768]{2,1,0:T(8,128)(2,1)S(1)}, bf16[6,384,768]{2,1,0:T(8,128)(2,1)}, u32[]{:S(2)}) %copy-start) | copy-done | bytes 3538968
  3.3 0.0 copy-start.1
  3.3 1.5 %copy-done.1 = bf16[6,384,384]{2,1,0:T(8,128)(2,1)S(1)} copy-done((bf16[6,384,384]{2,1,0:T(8,128)(2,1)S(1)}, bf16[6,384,384]{2,1,0:T(8,128)(2,1)}, u32[]{:S(2)}) %copy-start.1) | copy-done | bytes 1769496
  4.8 0.0 copy-start.2
  4.8 0.7 copy-done.2
  5.5 0.0 copy-start.3
  5.5 0.7 copy-done.3
  6.2 0.0 copy-start.4
  6.2 0.7 copy-done.4
  6.8 0.0 copy-start.5
  6.8 0.7 copy-done.5
  7.5 0.0 copy-start.6
  7.5 0.7 copy-done.6
  8.2 0.0 copy-start.7
  8.2 0.7 copy-done.7
  8.9 9.3 %condense_pack.1 = bf16[128,264,128]{2,1,0:T(8,128)(2,1)} custom-call(s32[1]{0:T(128)S(6)} %copy.12.counts, s32[6,1,36]{2,1,0:T(1,128)S(1)} %bitcast.2, s32[6,36]{1,0:T(8,128)S(1)} %copy-done.4, s32[6,1,6]{2,1,0:T(1,128)S(1)} %bitcast.3, s32[6,6]{1,0:T(8,128)S(1)} %copy-done.5, bf16[6,384,384]{2,1,0:T(8,128)(2,1)S(1)} %copy-done.1, ...), custom_call_target="tpu_custom_call" | custom-call | tf_op jit(solution)/shard_map/condense_pack/pallas_call | solution.py:151
  18.2 119.3 %all_to_all.5.got = bf16[128,264,128]{2,1,0:T(8,128)(2,1)} all-to-all(bf16[128,264,128]{2,1,0:T(8,128)(2,1)} %condense_pack.1), channel_id=1, replica_groups=mesh['grp'=4,'blk'=32] {'grp','blk'}, dimensions={0} | all-to-all | bytes 17301504 | tf_op jit(solution)/shard_map/all_to_all | solution.py:285
  137.4 10.0 %sum_tiles.1 = (f32[64,128,128]{2,1,0:T(8,128)}, f32[16,128]{1,0:T(8,128)}) custom-call(bf16[128,264,128]{2,1,0:T(8,128)(2,1)} %all_to_all.5.got), custom_call_target="tpu_custom_call" | custom-call | tf_op jit(solution)/shard_map/sum_tiles/pallas_call | solution.py:246
Async XLA Ops:
  1.3 2.0 %copy-start = (bf16[6,384,768]{2,1,0:T(8,128)(2,1)S(1)}, bf16[6,384,768]{2,1,0:T(8,128)(2,1)}, u32[]{:S(2)}) copy-start(bf16[6,384,768]{2,1,0:T(8,128)(2,1)} %couple_hbm.1) | copy-start | bytes 10616836
  3.3 1.5 %copy-start.1 = (bf16[6,384,384]{2,1,0:T(8,128)(2,1)S(1)}, bf16[6,384,384]{2,1,0:T(8,128)(2,1)}, u32[]{:S(2)}) copy-start(bf16[6,384,384]{2,1,0:T(8,128)(2,1)} %factor_hbm.1) | copy-start | bytes 5308420
  4.8 0.7 copy-start.2
  5.5 0.7 copy-start.3
  6.2 0.7 copy-start.4
  6.8 0.7 copy-start.5
  7.5 0.7 copy-start.6
  8.2 0.7 copy-start.7

commit v2 on v1

--- a/solution.py
+++ b/solution.py
@@ -10,6 +10,7 @@
 VSLOT_DEV = 16
 CAP = 2
 HEAD = 8
+WIDE = 256
 AXES = ("grp", "blk")
 MIB = 1 << 20
 
@@ -26,35 +27,53 @@
 
 def pack_kernel(
     counts,
+    owner_hbm,
+    slot_hbm,
+    vowner_hbm,
+    vslot_hbm,
+    factor_hbm,
+    couple_hbm,
+    bound_hbm,
+    inner_hbm,
+    outer_hbm,
+    send,
     owner,
     slot,
     vowner,
     vslot,
-    factor_hbm,
-    couple_hbm,
-    bound_hbm,
     inner,
     outer,
-    send,
     factor,
     couple,
     bound,
-    pieces,
     left,
     head,
-    head16,
     used,
     vused,
     target,
     vtarget,
+    table_sem,
     in_sem,
-    out_sem,
-    head_sem,
 ):
     emax, ni, nb = couple.shape
     tiles = nb // TILE
     per = tiles * tiles
     peers = used.shape[0]
+    tables = [
+        pltpu.make_async_copy(source, held, table_sem.at[i])
+        for i, (source, held) in enumerate(
+            (
+                (owner_hbm, owner),
+                (slot_hbm, slot),
+                (vowner_hbm, vowner),
+                (vslot_hbm, vslot),
+                (inner_hbm, inner),
+                (outer_hbm, outer),
+            )
+        )
+    ]
+    for copy in tables:
+        copy.start()
     live = counts[0]
 
     def loads(k):
@@ -77,6 +96,9 @@
         used[p] = 0
         vused[p] = 0
         head[pl.ds(pl.multiple_of(p * HEAD, HEAD), HEAD), :] = blank
+
+    for copy in tables:
+        copy.wait()
 
     @pl.loop(0, live)
     def _(k):
@@ -107,82 +129,65 @@
         pulled = lax.dot_general(
             inner_rows, factor[k], (((1,), (1,)), ((), ())), preferred_element_type=jnp.float32
         ).astype(jnp.bfloat16)
+        outer_rows = row_of(outer, k)
         left[pl.ds(0, nb), :] = coupled
         left[pl.ds(nb, 16), :] = pulled
-        for a in range(tiles):
-            last = a == tiles - 1
-            lhs = left[pl.ds(a * TILE, TILE + (16 if last else 0)), :]
+        for n in range(nb // WIDE):
             product = lax.dot_general(
-                lhs, left[pl.ds(0, nb), :], (((1,), (1,)), ((), ())), preferred_element_type=jnp.float32
+                left[...],
+                left[pl.ds(n * WIDE, WIDE), :],
+                (((1,), (1,)), ((), ())),
+                preferred_element_type=jnp.float32,
             )
-            schur = bound[k, pl.ds(a * TILE, TILE), :].astype(jnp.float32) - product[:TILE]
-            for b in range(tiles):
-                pieces[k, a * tiles + b] = schur[:, b * TILE : (b + 1) * TILE].astype(jnp.bfloat16)
-                t = k * per + a * tiles + b
-                to = target[t]
-                peer = lax.shift_right_logical(to, 1)
-                start = pl.multiple_of(HEAD + (to & 1) * TILE, HEAD)
-                pltpu.make_async_copy(
-                    pieces.at[k, a * tiles + b], send.at[peer, pl.ds(start, TILE), :], out_sem.at[k]
-                ).start()
-            if last:
-                condensed = row_of(outer, k) - product[TILE : TILE + 1]
-                for b in range(tiles):
-                    head[pl.ds(vtarget[k * tiles + b], 1), :] = condensed[:, b * TILE : (b + 1) * TILE]
-
-    head16[...] = head[...].reshape(peers, HEAD, TILE).astype(jnp.bfloat16)
-    head_copy = pltpu.make_async_copy(head16, send.at[:, pl.ds(0, HEAD), :], head_sem)
-    head_copy.start()
-
-    @pl.loop(0, live)
-    def _(k):
-        pltpu.make_async_copy(pieces.at[k], pieces.at[k], out_sem.at[k]).wait()
-
-    head_copy.wait()
+            for a in range(tiles):
+                rows = pl.ds(a * TILE, TILE)
+                schur = bound[k, rows, pl.ds(n * WIDE, WIDE)].astype(jnp.float32) - product[a * TILE : (a + 1) * TILE]
+                for b in range(WIDE // TILE):
+                    to = target[k * per + a * tiles + n * (WIDE // TILE) + b]
+                    peer = lax.shift_right_logical(to, 1)
+                    start = pl.multiple_of(HEAD + (to & 1) * TILE, HEAD)
+                    send[peer, pl.ds(start, TILE), :] = schur[:, b * TILE : (b + 1) * TILE].astype(jnp.bfloat16)
+            condensed = outer_rows[:, n * WIDE : (n + 1) * WIDE] - product[nb : nb + 1]
+            for b in range(WIDE // TILE):
+                at = vtarget[k * tiles + n * (WIDE // TILE) + b]
+                head[pl.ds(at, 1), :] = condensed[:, b * TILE : (b + 1) * TILE]
+
+    send[:, pl.ds(0, HEAD), :] = head[...].reshape(peers, HEAD, TILE).astype(jnp.bfloat16)
 
 
 def packed(peers, inv_factor, coupling, boundary, load_int, load_bnd, counts, owner, slot, vowner, vslot):
     emax, ni, nb = coupling.shape
     tiles = nb // TILE
     per = tiles * tiles
-    smem = pl.BlockSpec(memory_space=pltpu.SMEM)
     hbm = pl.BlockSpec(memory_space=pltpu.HBM)
-    vmem = pl.BlockSpec(memory_space=pltpu.VMEM)
+    operands = (owner, slot, vowner, vslot, inv_factor, coupling, boundary, load_int, load_bnd)
     return pl.pallas_call(
         pack_kernel,
-        out_shape=jax.ShapeDtypeStruct((peers, HEAD + CAP * TILE, TILE), jnp.bfloat16),
-        in_specs=[smem] * 5 + [hbm] * 3 + [vmem] * 2,
-        out_specs=hbm,
+        out_shape=pltpu.VMEM((peers, HEAD + CAP * TILE, TILE), jnp.bfloat16),
+        in_specs=[pl.BlockSpec(memory_space=pltpu.SMEM)] + [hbm] * len(operands),
+        out_specs=pl.BlockSpec(memory_space=pltpu.VMEM),
         scratch_shapes=[
+            pltpu.SMEM((emax, 1, per), jnp.int32),
+            pltpu.SMEM((emax, per), jnp.int32),
+            pltpu.SMEM((emax, 1, tiles), jnp.int32),
+            pltpu.SMEM((emax, tiles), jnp.int32),
+            pltpu.VMEM((emax, ni), jnp.bfloat16),
+            pltpu.VMEM((emax, nb), jnp.bfloat16),
             pltpu.VMEM((emax, ni, ni), jnp.bfloat16),
             pltpu.VMEM((emax, ni, nb), jnp.bfloat16),
             pltpu.VMEM((emax, nb, nb), jnp.bfloat16),
-            pltpu.VMEM((emax, per, TILE, TILE), jnp.bfloat16),
             pltpu.VMEM((nb + 16, ni), jnp.bfloat16),
             pltpu.VMEM((peers * HEAD, TILE), jnp.float32),
-            pltpu.VMEM((peers, HEAD, TILE), jnp.bfloat16),
             pltpu.SMEM((peers,), jnp.int32),
             pltpu.SMEM((peers,), jnp.int32),
             pltpu.SMEM((emax * per,), jnp.int32),
             pltpu.SMEM((emax * tiles,), jnp.int32),
+            pltpu.SemaphoreType.DMA((6,)),
             pltpu.SemaphoreType.DMA((3, emax)),
-            pltpu.SemaphoreType.DMA((emax,)),
-            pltpu.SemaphoreType.DMA,
         ],
         compiler_params=pltpu.CompilerParams(vmem_limit_bytes=48 * MIB),
         name="condense_pack",
-    )(
-        counts,
-        owner,
-        slot,
-        vowner,
-        vslot,
-        inv_factor,
-        coupling,
-        boundary,
-        load_int,
-        load_bnd,
-    )
+    )(counts, *(pltpu.with_memory_space_constraint(x, pltpu.HBM) for x in operands))
 
 
 def sum_kernel(got, assembled, loads, head, parts, ids_vec, ids, head_sem, part_sem, ids_sem):
@@ -262,7 +267,7 @@
         ],
         compiler_params=pltpu.CompilerParams(vmem_limit_bytes=48 * MIB),
         name="sum_tiles",
-    )(got)
+    )(pltpu.with_memory_space_constraint(got, pltpu.HBM))
 
 
 def shards(

time: 149 us -> 137 us (0.919)
  local copies, waits for them, and re-layouts: 7.61 us -> 0 us
  blocking collectives: 119 us -> 113 us
  Pallas kernels: 19.2 us -> 21.7 us
    unnamed x16 -> x0, local copies, waits for them, and re-layouts: 7.61 us -> none
    all_to_all x1, blocking collectives: 119 us -> 113 us  [shards(): got = lax.all_to_all(send, AXES, split_axis=0, concat_axis=0, tiled=True)]
    pallas_call x1, Pallas kernels: 9.25 us -> 11.7 us  [packed(): pl.pallas_call(pack_kernel, out_shape=pltpu.VMEM((peers, HEAD + CAP * TIL...]
where the time goes in v2:
time: 137 us; the launch traced here: 136 us
  blocking collectives  113 us (82%)
  Pallas kernels  21.7 us (16%)
    all_to_all x1, blocking collectives, shards(): got = lax.all_to_all(send, AXES, split_axis=0, concat_axis=0, tiled=True)  113 us
    pallas_call x1, Pallas kernels, packed(): pl.pallas_call(pack_kernel, out_shape=pltpu.VMEM((peers, HEAD + CAP * TIL...  11.7 us
    pallas_call x1, Pallas kernels, summed(): pl.pallas_call(sum_kernel, out_shape=(jax.ShapeDtypeStruct((SLOT_DEV, TIL...  10 us

profile of v2, /device:TPU:0, one launch (start us, length us, event | category | flops | bytes accessed | tf_op | source)
XLA Modules:
  0.0 135.5 jit_solution(2414779678781184422)
XLA Ops:
  1.3 11.7 %condense_pack.1 = bf16[128,264,128]{2,1,0:T(8,128)(2,1)S(1)} custom-call(s32[1]{0:T(128)S(6)} %copy.12.counts, s32[6,1,36]{2,1,0:T(1,128)} %bitcast.2, s32[6,36]{1,0:T(8,128)} %slot_hbm.1, s32[6,1,6]{2,1,0:T(1,128)} %bitcast.3, s32[6,6]{1,0:T(8,128)} %vslot_hbm.1, bf16[6,384,384]{2,1,0:T(8,128)(2,1)} %factor_hbm.1, bf16[6,384,768]{2,1,0:T(8,128)(2,1)} %couple_hbm.1, ...), custom_call_target="tpu_custom_call" | custom-call | tf_op jit(solution)/shard_map/condense_pack/pallas_call | solution.py:164
  13.0 112.5 %all_to_all.5.got = bf16[128,264,128]{2,1,0:T(8,128)(2,1)} all-to-all(bf16[128,264,128]{2,1,0:T(8,128)(2,1)S(1)} %condense_pack.1), channel_id=1, replica_groups=mesh['grp'=4,'blk'=32] {'grp','blk'}, dimensions={0} | all-to-all | bytes 17301504 | tf_op jit(solution)/shard_map/all_to_all | solution.py:290
  125.5 10.0 %sum_tiles.1 = (f32[64,128,128]{2,1,0:T(8,128)}, f32[16,128]{1,0:T(8,128)}) custom-call(bf16[128,264,128]{2,1,0:T(8,128)(2,1)} %all_to_all.5.got), custom_call_target="tpu_custom_call" | custom-call | tf_op jit(solution)/shard_map/sum_tiles/pallas_call | solution.py:251

commit v3 on v2

--- a/solution.py
+++ b/solution.py
@@ -1,3 +1,5 @@
+import functools
+
 import jax
 import jax.numpy as jnp
 from jax import lax
@@ -26,6 +28,7 @@
 
 
 def pack_kernel(
+    columns,
     counts,
     owner_hbm,
     slot_hbm,
@@ -76,6 +79,9 @@
         copy.start()
     live = counts[0]
 
+    def place_of(device):
+        return lax.rem(device, columns) * (peers // columns) + lax.div(device, columns)
+
     def loads(k):
         return (
             pltpu.make_async_copy(factor_hbm.at[k], factor.at[k], in_sem.at[0, k]),
@@ -104,7 +110,7 @@
     def _(k):
         @pl.loop(0, per)
         def _(t):
-            p = owner[k, 0, t]
+            p = place_of(owner[k, 0, t])
             r = used[p]
             used[p] = r + 1
             target[k * per + t] = p * CAP + r
@@ -112,7 +118,7 @@
 
         @pl.loop(0, tiles)
         def _(t):
-            p = vowner[k, 0, t]
+            p = place_of(vowner[k, 0, t])
             r = vused[p]
             vused[p] = r + 1
             vtarget[k * tiles + t] = p * HEAD + r
@@ -155,14 +161,14 @@
     send[:, pl.ds(0, HEAD), :] = head[...].reshape(peers, HEAD, TILE).astype(jnp.bfloat16)
 
 
-def packed(peers, inv_factor, coupling, boundary, load_int, load_bnd, counts, owner, slot, vowner, vslot):
+def packed(columns, peers, inv_factor, coupling, boundary, load_int, load_bnd, counts, owner, slot, vowner, vslot):
     emax, ni, nb = coupling.shape
     tiles = nb // TILE
     per = tiles * tiles
     hbm = pl.BlockSpec(memory_space=pltpu.HBM)
     operands = (owner, slot, vowner, vslot, inv_factor, coupling, boundary, load_int, load_bnd)
     return pl.pallas_call(
-        pack_kernel,
+        functools.partial(pack_kernel, columns),
         out_shape=pltpu.VMEM((peers, HEAD + CAP * TILE, TILE), jnp.bfloat16),
         in_specs=[pl.BlockSpec(memory_space=pltpu.SMEM)] + [hbm] * len(operands),
         out_specs=pl.BlockSpec(memory_space=pltpu.VMEM),
@@ -190,34 +196,37 @@
     )(counts, *(pltpu.with_memory_space_constraint(x, pltpu.HBM) for x in operands))
 
 
-def sum_kernel(got, assembled, loads, head, parts, ids_vec, ids, head_sem, part_sem, ids_sem):
+def sum_kernel(got, assembled, loads, total, head, parts, ids_vec, ids, head_sem, part_sem, ids_sem, out_sem):
     peers = head.shape[0]
     chunks, width = parts.shape[:2]
+
+    def part_copy(c):
+        return pltpu.make_async_copy(
+            got.at[pl.ds(c * width, width), pl.ds(HEAD, CAP * TILE), :], parts.at[c], part_sem.at[c]
+        )
+
     head_copy = pltpu.make_async_copy(got.at[:, pl.ds(0, HEAD), :], head, head_sem)
     head_copy.start()
-    for c in range(chunks):
-        pltpu.make_async_copy(
-            got.at[pl.ds(c * width, width), pl.ds(HEAD, CAP * TILE), :], parts.at[c], part_sem.at[c]
-        ).start()
-
     zero = jnp.zeros((TILE, TILE), jnp.float32)
 
     @pl.loop(0, SLOT_DEV)
     def _(s):
-        assembled[s] = zero
+        total[s] = zero
 
     head_copy.wait()
+    for c in range(chunks):
+        part_copy(c).start()
     rows = head[...].astype(jnp.float32)
     diagonal = lax.broadcasted_iota(jnp.int32, (peers, TILE), 0) == lax.broadcasted_iota(
         jnp.int32, (peers, TILE), 1
     )
     lane = lax.broadcasted_iota(jnp.int32, (peers, TILE), 1).astype(jnp.float32)
-    total = jnp.zeros((TILE, TILE), jnp.float32)
+    vec = jnp.zeros((TILE, TILE), jnp.float32)
     for r in range(CAP):
-        named = jnp.where(diagonal, rows[:, CAP + r, :], 0.0)
+        named = jnp.where(diagonal, jnp.where(rows[:, CAP + r, :] < 0, SLOT_DEV * 1.0, rows[:, CAP + r, :]), 0.0)
         ids_vec[pl.ds(r, 1), :] = jnp.sum(named, axis=0, keepdims=True).astype(jnp.int32)
         select = (rows[:, 2 * CAP + r, :] == lane).astype(jnp.bfloat16)
-        total += lax.dot_general(
+        vec += lax.dot_general(
             select,
             rows[:, r, :].astype(jnp.bfloat16),
             (((0,), (0,)), ((), ())),
@@ -225,22 +234,21 @@
         )
     ids_copy = pltpu.make_async_copy(ids_vec, ids, ids_sem)
     ids_copy.start()
-    loads[...] = total[:VSLOT_DEV]
+    loads[...] = vec[:VSLOT_DEV]
     ids_copy.wait()
 
     for c in range(chunks):
-        pltpu.make_async_copy(
-            got.at[pl.ds(c * width, width), pl.ds(HEAD, CAP * TILE), :], parts.at[c], part_sem.at[c]
-        ).wait()
+        part_copy(c).wait()
 
         @pl.loop(0, width)
         def _(w):
             for r in range(CAP):
                 s = ids[r, c * width + w]
-
-                @pl.when(s >= 0)
-                def _():
-                    assembled[s] += parts[c, w, pl.ds(r * TILE, TILE), :].astype(jnp.float32)
+                total[s] += parts[c, w, pl.ds(r * TILE, TILE), :].astype(jnp.float32)
+
+    out_copy = pltpu.make_async_copy(total.at[pl.ds(0, SLOT_DEV)], assembled, out_sem)
+    out_copy.start()
+    out_copy.wait()
 
 
 def summed(got):
@@ -255,8 +263,9 @@
             jax.ShapeDtypeStruct((VSLOT_DEV, TILE), jnp.float32),
         ),
         in_specs=[hbm],
-        out_specs=(vmem, vmem),
+        out_specs=(hbm, vmem),
         scratch_shapes=[
+            pltpu.VMEM((SLOT_DEV + 1, TILE, TILE), jnp.float32),
             pltpu.VMEM((peers, HEAD, TILE), jnp.bfloat16),
             pltpu.VMEM((chunks, peers // chunks, CAP * TILE, TILE), jnp.bfloat16),
             pltpu.VMEM((8, TILE), jnp.int32),
@@ -264,6 +273,7 @@
             pltpu.SemaphoreType.DMA,
             pltpu.SemaphoreType.DMA((chunks,)),
             pltpu.SemaphoreType.DMA,
+            pltpu.SemaphoreType.DMA,
         ],
         compiler_params=pltpu.CompilerParams(vmem_limit_bytes=48 * MIB),
         name="sum_tiles",
@@ -275,6 +285,7 @@
 ):
     peers = lax.axis_size("grp") * lax.axis_size("blk")
     send = packed(
+        lax.axis_size("blk"),
         peers,
         inv_factor,
         coupling,
@@ -287,7 +298,7 @@
         jnp.swapaxes(vec_owner, 1, 2),
         vec_slot,
     )
-    got = lax.all_to_all(send, AXES, split_axis=0, concat_axis=0, tiled=True)
+    got = lax.all_to_all(send, ("blk", "grp"), split_axis=0, concat_axis=0, tiled=True)
     return summed(got)
 
 

time: 137 us -> 134 us (0.978)
  Pallas kernels: 21.7 us -> 12.3 us
  blocking collectives: 113 us -> 119 us
    all_to_all x1, blocking collectives: 113 us -> 119 us  [shards(): lax.all_to_all(send, ('blk', 'grp'), split_axis=0, concat_axis=0, tiled=T...]
    pallas_call x1, Pallas kernels: 11.7 us -> 4.97 us  [packed(): pl.pallas_call(functools.partial(pack_kernel, columns), out_shape=pltpu.V...]
    pallas_call x1, Pallas kernels: 10 us -> 7.35 us  [summed(): pl.pallas_call(sum_kernel, out_shape=(jax.ShapeDtypeStruct((SLOT_DEV, TIL...]
where the time goes in v3:
time: 134 us; the launch traced here: 133 us
  blocking collectives  119 us (89%)
  Pallas kernels  12.3 us (9%)
    all_to_all x1, blocking collectives, shards(): lax.all_to_all(send, ('blk', 'grp'), split_axis=0, concat_axis=0, tiled=T...  119 us
    pallas_call x1, Pallas kernels, summed(): pl.pallas_call(sum_kernel, out_shape=(jax.ShapeDtypeStruct((SLOT_DEV, TIL...  7.35 us
    pallas_call x1, Pallas kernels, packed(): pl.pallas_call(functools.partial(pack_kernel, columns), out_shape=pltpu.V...  4.97 us

profile of v3, /device:TPU:0, one launch (start us, length us, event | category | flops | bytes accessed | tf_op | source)
XLA Modules:
  0.0 133.0 jit_solution(9793838119723045344)
XLA Ops:
  1.3 5.0 %condense_pack.1 = bf16[128,264,128]{2,1,0:T(8,128)(2,1)S(1)} custom-call(s32[1]{0:T(128)S(6)} %copy.12.counts, s32[6,1,36]{2,1,0:T(1,128)} %bitcast.2, s32[6,36]{1,0:T(8,128)} %slot_hbm.1, s32[6,1,6]{2,1,0:T(1,128)} %bitcast.3, s32[6,6]{1,0:T(8,128)} %vslot_hbm.1, bf16[6,384,384]{2,1,0:T(8,128)(2,1)} %factor_hbm.1, bf16[6,384,768]{2,1,0:T(8,128)(2,1)} %couple_hbm.1, ...), custom_call_target="tpu_custom_call" | custom-call | tf_op jit(solution)/shard_map/condense_pack/pallas_call | solution.py:170
  6.3 119.4 %all_to_all.5.got = bf16[128,264,128]{2,1,0:T(8,128)(2,1)} all-to-all(bf16[128,264,128]{2,1,0:T(8,128)(2,1)S(1)} %condense_pack.1), channel_id=1, replica_groups=mesh['grp'=4,'blk'=32] {'blk','grp'}, dimensions={0} | all-to-all | bytes 17301504 | tf_op jit(solution)/shard_map/all_to_all | solution.py:301
  125.7 7.3 %sum_tiles.1 = (f32[64,128,128]{2,1,0:T(8,128)}, f32[16,128]{1,0:T(8,128)}) custom-call(bf16[128,264,128]{2,1,0:T(8,128)(2,1)} %all_to_all.5.got), custom_call_target="tpu_custom_call" | custom-call | tf_op jit(solution)/shard_map/sum_tiles/pallas_call | solution.py:259

commit v4 on v3

--- a/solution.py
+++ b/solution.py
@@ -53,8 +53,6 @@
     head,
     used,
     vused,
-    target,
-    vtarget,
     table_sem,
     in_sem,
 ):
@@ -80,7 +78,8 @@
     live = counts[0]
 
     def place_of(device):
-        return lax.rem(device, columns) * (peers // columns) + lax.div(device, columns)
+        shift = columns.bit_length() - 1
+        return (device & (columns - 1)) * (peers // columns) + lax.shift_right_logical(device, shift)
 
     def loads(k):
         return (
@@ -105,24 +104,6 @@
 
     for copy in tables:
         copy.wait()
-
-    @pl.loop(0, live)
-    def _(k):
-        @pl.loop(0, per)
-        def _(t):
-            p = place_of(owner[k, 0, t])
-            r = used[p]
-            used[p] = r + 1
-            target[k * per + t] = p * CAP + r
-            head[pl.ds(p * HEAD + CAP + r, 1), :] = spread(slot[k, t])
-
-        @pl.loop(0, tiles)
-        def _(t):
-            p = place_of(vowner[k, 0, t])
-            r = vused[p]
-            vused[p] = r + 1
-            vtarget[k * tiles + t] = p * HEAD + r
-            head[pl.ds(p * HEAD + 2 * CAP + r, 1), :] = spread(vslot[k, t])
 
     @pl.loop(0, live)
     def _(k):
@@ -149,14 +130,21 @@
                 rows = pl.ds(a * TILE, TILE)
                 schur = bound[k, rows, pl.ds(n * WIDE, WIDE)].astype(jnp.float32) - product[a * TILE : (a + 1) * TILE]
                 for b in range(WIDE // TILE):
-                    to = target[k * per + a * tiles + n * (WIDE // TILE) + b]
-                    peer = lax.shift_right_logical(to, 1)
-                    start = pl.multiple_of(HEAD + (to & 1) * TILE, HEAD)
-                    send[peer, pl.ds(start, TILE), :] = schur[:, b * TILE : (b + 1) * TILE].astype(jnp.bfloat16)
+                    t = a * tiles + n * (WIDE // TILE) + b
+                    p = place_of(owner[k, 0, t])
+                    r = used[p]
+                    used[p] = r + 1
+                    head[pl.ds(p * HEAD + CAP + r, 1), :] = spread(slot[k, t])
+                    start = pl.multiple_of(HEAD + r * TILE, HEAD)
+                    send[p, pl.ds(start, TILE), :] = schur[:, b * TILE : (b + 1) * TILE].astype(jnp.bfloat16)
             condensed = outer_rows[:, n * WIDE : (n + 1) * WIDE] - product[nb : nb + 1]
             for b in range(WIDE // TILE):
-                at = vtarget[k * tiles + n * (WIDE // TILE) + b]
-                head[pl.ds(at, 1), :] = condensed[:, b * TILE : (b + 1) * TILE]
+                t = n * (WIDE // TILE) + b
+                p = place_of(vowner[k, 0, t])
+                r = vused[p]
+                vused[p] = r + 1
+                head[pl.ds(p * HEAD + r, 1), :] = condensed[:, b * TILE : (b + 1) * TILE]
+                head[pl.ds(p * HEAD + 2 * CAP + r, 1), :] = spread(vslot[k, t])
 
     send[:, pl.ds(0, HEAD), :] = head[...].reshape(peers, HEAD, TILE).astype(jnp.bfloat16)
 
@@ -186,8 +174,6 @@
             pltpu.VMEM((peers * HEAD, TILE), jnp.float32),
             pltpu.SMEM((peers,), jnp.int32),
             pltpu.SMEM((peers,), jnp.int32),
-            pltpu.SMEM((emax * per,), jnp.int32),
-            pltpu.SMEM((emax * tiles,), jnp.int32),
             pltpu.SemaphoreType.DMA((6,)),
             pltpu.SemaphoreType.DMA((3, emax)),
         ],

time: 134 us -> 131 us (0.978)
  blocking collectives: 119 us -> 116 us
    all_to_all x1, blocking collectives: 119 us -> 116 us  [shards(): lax.all_to_all(send, ('blk', 'grp'), split_axis=0, concat_axis=0, tiled=T...]
where the time goes in v4:
time: 131 us; the launch traced here: 130 us
  blocking collectives  116 us (89%)
  Pallas kernels  13.1 us (10%)
    all_to_all x1, blocking collectives, shards(): lax.all_to_all(send, ('blk', 'grp'), split_axis=0, concat_axis=0, tiled=T...  116 us
    pallas_call x1, Pallas kernels, summed(): pl.pallas_call(sum_kernel, out_shape=(jax.ShapeDtypeStruct((SLOT_DEV, TIL...  7.34 us
    pallas_call x1, Pallas kernels, packed(): pl.pallas_call(functools.partial(pack_kernel, columns), out_shape=pltpu.V...  5.73 us

profile of v4, /device:TPU:0, one launch (start us, length us, event | category | flops | bytes accessed | tf_op | source)
XLA Modules:
  0.0 130.1 jit_solution(8796908237338676350)
XLA Ops:
  1.3 5.7 %condense_pack.1 = bf16[128,264,128]{2,1,0:T(8,128)(2,1)S(1)} custom-call(s32[1]{0:T(128)S(6)} %copy.12.counts, s32[6,1,36]{2,1,0:T(1,128)} %bitcast.2, s32[6,36]{1,0:T(8,128)} %slot_hbm.1, s32[6,1,6]{2,1,0:T(1,128)} %bitcast.3, s32[6,6]{1,0:T(8,128)} %vslot_hbm.1, bf16[6,384,384]{2,1,0:T(8,128)(2,1)} %factor_hbm.1, bf16[6,384,768]{2,1,0:T(8,128)(2,1)} %couple_hbm.1, ...), custom_call_target="tpu_custom_call" | custom-call | tf_op jit(solution)/shard_map/condense_pack/pallas_call | solution.py:158
  7.0 115.7 %all_to_all.5.got = bf16[128,264,128]{2,1,0:T(8,128)(2,1)} all-to-all(bf16[128,264,128]{2,1,0:T(8,128)(2,1)S(1)} %condense_pack.1), channel_id=1, replica_groups=mesh['grp'=4,'blk'=32] {'blk','grp'}, dimensions={0} | all-to-all | bytes 17301504 | tf_op jit(solution)/shard_map/all_to_all | solution.py:287
  122.7 7.3 %sum_tiles.1 = (f32[64,128,128]{2,1,0:T(8,128)}, f32[16,128]{1,0:T(8,128)}) custom-call(bf16[128,264,128]{2,1,0:T(8,128)(2,1)} %all_to_all.5.got), custom_call_target="tpu_custom_call" | custom-call | tf_op jit(solution)/shard_map/sum_tiles/pallas_call | solution.py:245

commit v5 on v4

--- a/solution.py
+++ b/solution.py
@@ -11,6 +11,7 @@
 SLOT_DEV = 64
 VSLOT_DEV = 16
 CAP = 2
+EXTRA = 16
 HEAD = 8
 WIDE = 256
 AXES = ("grp", "blk")
@@ -119,25 +120,32 @@
         outer_rows = row_of(outer, k)
         left[pl.ds(0, nb), :] = coupled
         left[pl.ds(nb, 16), :] = pulled
+        def put(a, b, product):
+            t = a * tiles + b
+            schur = bound[k, pl.ds(a * TILE, TILE), pl.ds(b * TILE, TILE)].astype(jnp.float32) - product
+            p = place_of(owner[k, 0, t])
+            r = used[p]
+            used[p] = r + 1
+            head[pl.ds(p * HEAD + CAP + r, 1), :] = spread(slot[k, t])
+            start = pl.multiple_of(HEAD + r * TILE, HEAD)
+            send[p, pl.ds(start, TILE), :] = schur.astype(jnp.bfloat16)
+
+        wide = WIDE // TILE
         for n in range(nb // WIDE):
+            above = n * WIDE
             product = lax.dot_general(
-                left[...],
-                left[pl.ds(n * WIDE, WIDE), :],
+                left[pl.ds(above, nb + EXTRA - above), :],
+                left[pl.ds(above, WIDE), :],
                 (((1,), (1,)), ((), ())),
                 preferred_element_type=jnp.float32,
             )
-            for a in range(tiles):
-                rows = pl.ds(a * TILE, TILE)
-                schur = bound[k, rows, pl.ds(n * WIDE, WIDE)].astype(jnp.float32) - product[a * TILE : (a + 1) * TILE]
-                for b in range(WIDE // TILE):
-                    t = a * tiles + n * (WIDE // TILE) + b
-                    p = place_of(owner[k, 0, t])
-                    r = used[p]
-                    used[p] = r + 1
-                    head[pl.ds(p * HEAD + CAP + r, 1), :] = spread(slot[k, t])
-                    start = pl.multiple_of(HEAD + r * TILE, HEAD)
-                    send[p, pl.ds(start, TILE), :] = schur[:, b * TILE : (b + 1) * TILE].astype(jnp.bfloat16)
-            condensed = outer_rows[:, n * WIDE : (n + 1) * WIDE] - product[nb : nb + 1]
+            for a in range(n * wide, tiles):
+                for b in range(wide):
+                    block = product[a * TILE - above : (a + 1) * TILE - above, b * TILE : (b + 1) * TILE]
+                    put(a, n * wide + b, block)
+                    if a >= (n + 1) * wide:
+                        put(n * wide + b, a, block.T)
+            condensed = outer_rows[:, n * WIDE : (n + 1) * WIDE] - product[nb - above : nb + 1 - above]
             for b in range(WIDE // TILE):
                 t = n * (WIDE // TILE) + b
                 p = place_of(vowner[k, 0, t])

time: 131 us -> 130 us (level)
  no operation moved by 1% of the time
where the time goes in v5:
time: 130 us; the launch traced here: 129 us
  blocking collectives  115 us (88%)
  Pallas kernels  12.7 us (10%)
    all_to_all x1, blocking collectives, shards(): lax.all_to_all(send, ('blk', 'grp'), split_axis=0, concat_axis=0, tiled=T...  115 us
    pallas_call x1, Pallas kernels, summed(): pl.pallas_call(sum_kernel, out_shape=(jax.ShapeDtypeStruct((SLOT_DEV, TIL...  7.34 us
    pallas_call x1, Pallas kernels, packed(): pl.pallas_call(functools.partial(pack_kernel, columns), out_shape=pltpu.V...  5.32 us

profile of v5, /device:TPU:0, one launch (start us, length us, event | category | flops | bytes accessed | tf_op | source)
XLA Modules:
  0.0 128.8 jit_solution(17750297302239615616)
XLA Ops:
  1.3 5.3 %condense_pack.1 = bf16[128,264,128]{2,1,0:T(8,128)(2,1)S(1)} custom-call(s32[1]{0:T(128)S(6)} %copy.12.counts, s32[6,1,36]{2,1,0:T(1,128)} %bitcast.2, s32[6,36]{1,0:T(8,128)} %slot_hbm.1, s32[6,1,6]{2,1,0:T(1,128)} %bitcast.3, s32[6,6]{1,0:T(8,128)} %vslot_hbm.1, bf16[6,384,384]{2,1,0:T(8,128)(2,1)} %factor_hbm.1, bf16[6,384,768]{2,1,0:T(8,128)(2,1)} %couple_hbm.1, ...), custom_call_target="tpu_custom_call" | custom-call | tf_op jit(solution)/shard_map/condense_pack/pallas_call | solution.py:166
  6.6 114.9 %all_to_all.5.got = bf16[128,264,128]{2,1,0:T(8,128)(2,1)} all-to-all(bf16[128,264,128]{2,1,0:T(8,128)(2,1)S(1)} %condense_pack.1), channel_id=1, replica_groups=mesh['grp'=4,'blk'=32] {'blk','grp'}, dimensions={0} | all-to-all | bytes 17301504 | tf_op jit(solution)/shard_map/all_to_all | solution.py:295
  121.5 7.3 %sum_tiles.1 = (f32[64,128,128]{2,1,0:T(8,128)}, f32[16,128]{1,0:T(8,128)}) custom-call(bf16[128,264,128]{2,1,0:T(8,128)(2,1)} %all_to_all.5.got), custom_call_target="tpu_custom_call" | custom-call | tf_op jit(solution)/shard_map/sum_tiles/pallas_call | solution.py:253

commit v6 on v5

--- a/solution.py
+++ b/solution.py
@@ -215,10 +215,13 @@
         jnp.int32, (peers, TILE), 1
     )
     lane = lax.broadcasted_iota(jnp.int32, (peers, TILE), 1).astype(jnp.float32)
+    for r in range(CAP):
+        named = jnp.where(rows[:, CAP + r, :] < 0, float(SLOT_DEV), rows[:, CAP + r, :])
+        ids_vec[pl.ds(r, 1), :] = jnp.sum(jnp.where(diagonal, named, 0.0), axis=0, keepdims=True).astype(jnp.int32)
+    ids_copy = pltpu.make_async_copy(ids_vec, ids, ids_sem)
+    ids_copy.start()
     vec = jnp.zeros((TILE, TILE), jnp.float32)
     for r in range(CAP):
-        named = jnp.where(diagonal, jnp.where(rows[:, CAP + r, :] < 0, SLOT_DEV * 1.0, rows[:, CAP + r, :]), 0.0)
-        ids_vec[pl.ds(r, 1), :] = jnp.sum(named, axis=0, keepdims=True).astype(jnp.int32)
         select = (rows[:, 2 * CAP + r, :] == lane).astype(jnp.bfloat16)
         vec += lax.dot_general(
             select,
@@ -226,15 +229,13 @@
             (((0,), (0,)), ((), ())),
             preferred_element_type=jnp.float32,
         )
-    ids_copy = pltpu.make_async_copy(ids_vec, ids, ids_sem)
-    ids_copy.start()
     loads[...] = vec[:VSLOT_DEV]
     ids_copy.wait()
 
     for c in range(chunks):
         part_copy(c).wait()
 
-        @pl.loop(0, width)
+        @pl.loop(0, width, unroll=4)
         def _(w):
             for r in range(CAP):
                 s = ids[r, c * width + w]

time: 130 us -> 130 us (level)
  Pallas kernels: 12.7 us -> 16.1 us
  blocking collectives: 115 us -> 112 us
    pallas_call x1, Pallas kernels: 5.32 us -> 8.82 us  [packed(): pl.pallas_call(functools.partial(pack_kernel, columns), out_shape=pltpu.V...]
    all_to_all x1, blocking collectives: 115 us -> 112 us  [shards(): lax.all_to_all(send, ('blk', 'grp'), split_axis=0, concat_axis=0, tiled=T...]
where the time goes in v6:
time: 130 us; the launch traced here: 129 us
  blocking collectives  112 us (86%)
  Pallas kernels  16.1 us (12%)
    all_to_all x1, blocking collectives, shards(): lax.all_to_all(send, ('blk', 'grp'), split_axis=0, concat_axis=0, tiled=T...  112 us
    pallas_call x1, Pallas kernels, packed(): pl.pallas_call(functools.partial(pack_kernel, columns), out_shape=pltpu.V...  8.82 us
    pallas_call x1, Pallas kernels, summed(): pl.pallas_call(sum_kernel, out_shape=(jax.ShapeDtypeStruct((SLOT_DEV, TIL...  7.3 us

profile of v6, /device:TPU:0, one launch (start us, length us, event | category | flops | bytes accessed | tf_op | source)
XLA Modules:
  0.0 129.2 jit_solution(14290120039247598622)
XLA Ops:
  1.3 8.8 %condense_pack.1 = bf16[128,264,128]{2,1,0:T(8,128)(2,1)S(1)} custom-call(s32[1]{0:T(128)S(6)} %copy.12.counts, s32[6,1,36]{2,1,0:T(1,128)} %bitcast.2, s32[6,36]{1,0:T(8,128)} %slot_hbm.1, s32[6,1,6]{2,1,0:T(1,128)} %bitcast.3, s32[6,6]{1,0:T(8,128)} %vslot_hbm.1, bf16[6,384,384]{2,1,0:T(8,128)(2,1)} %factor_hbm.1, bf16[6,384,768]{2,1,0:T(8,128)(2,1)} %couple_hbm.1, ...), custom_call_target="tpu_custom_call" | custom-call | tf_op jit(solution)/shard_map/condense_pack/pallas_call | solution.py:166
  10.1 111.8 %all_to_all.5.got = bf16[128,264,128]{2,1,0:T(8,128)(2,1)} all-to-all(bf16[128,264,128]{2,1,0:T(8,128)(2,1)S(1)} %condense_pack.1), channel_id=1, replica_groups=mesh['grp'=4,'blk'=32] {'blk','grp'}, dimensions={0} | all-to-all | bytes 17301504 | tf_op jit(solution)/shard_map/all_to_all | solution.py:296
  121.9 7.3 %sum_tiles.1 = (f32[64,128,128]{2,1,0:T(8,128)}, f32[16,128]{1,0:T(8,128)}) custom-call(bf16[128,264,128]{2,1,0:T(8,128)(2,1)} %all_to_all.5.got), custom_call_target="tpu_custom_call" | custom-call | tf_op jit(solution)/shard_map/sum_tiles/pallas_call | solution.py:254
